TPU v7x, 256 devices: a whole 4x4x8 slice. The times are simulated.
256 devices in a mesh: dp: 2 (over y_lo), ulysses: 8 (over x, core), blk: 16 (over y_hi, z).
Axes of the slice: x: 4, y: 4 (y_hi: 2, y_lo: 2; y = y_hi * 2 + y_lo), z: 8, core: 2. Of those that a mesh axis runs over, the one named last changes fastest.
Arguments:
- hidden_in: bfloat16 [2, 16384, 4096], P('dp', ('blk', 'ulysses')), may hold values from -6 to 6
- queries: bfloat16 [2, 16384, 2048], P('dp', ('blk', 'ulysses')), may hold values from -240 to 240
- pair_weight: bfloat16 [4096, 2048], P(('dp', 'blk')), may hold values from -0.09375 to 0.09375
- span_order: int32 [2, 32], P('dp'), may hold values from 0 to 31, each once within a row
- yarn_divisor: int32 [64], replicated, may hold values from 1 to 8
Outputs:
- attended: bfloat16 [2, 16384, 2048], P('dp', ('blk', 'ulysses'))
All inputs are finite; a program needn't handle non-finite values.
Results may differ from a plain program's by a relative error of at most 0.02.
The roundings to bfloat16 on the way count: a program that leaves them out, or rounds other values in their place, can miss the bound.
Values may be sent and summed in bfloat16 or wider, within the bound.
A program may use at most 128 MiB of HBM per device.

v0:
```python
import math
import jax
import jax.numpy as jnp
from jax import lax
from jax.sharding import PartitionSpec as P

KVH = 8
HD = 128
QH = 16
STEPS = 3
LOG_BASE = math.log(500000.0)


def from_behind(block, axis, distance):
    devices = range(lax.axis_size(axis))
    route = [((i - distance) % len(devices), i) for i in devices]
    return lax.ppermute(block, axis, route)


def rotate(vectors, angle_table):
    half_dim = vectors.shape[-1] // 2
    first_half = vectors[..., :half_dim]
    second_half = vectors[..., half_dim:]
    cosine = jnp.cos(angle_table)
    sine_part = jnp.sin(angle_table)
    return jnp.concatenate(
        [
            first_half * cosine - second_half * sine_part,
            second_half * cosine + first_half * sine_part,
        ],
        axis=-1,
    )


def angles(positions, yarn_divisor):
    half_dim = yarn_divisor.shape[0]
    scaled = 2.0 * jnp.arange(half_dim, dtype=jnp.float32) / (2 * half_dim)
    inverse = jnp.exp(-LOG_BASE * scaled) / yarn_divisor.astype(jnp.float32)
    return positions.astype(jnp.float32)[:, None] * inverse[None, :]


def positions_of(order_row, first_row, row_count, span_rows):
    stored = first_row + jnp.arange(row_count, dtype=jnp.int32)
    span_index = stored // span_rows
    matches = span_index[:, None] == jnp.arange(order_row.shape[0], dtype=jnp.int32)[None, :]
    span_value = jnp.sum(jnp.where(matches, order_row[None, :], 0), axis=1)
    return span_value * span_rows + stored % span_rows


def tile_scores(query_rows, key_rows):
    product = lax.dot_general(
        query_rows, key_rows, (((1,), (1,)), ((), ())), preferred_element_type=jnp.float32
    )
    return product * (1.0 / math.sqrt(HD))


def row_maximum(query_rows, query_pos, key_rows, key_pos):
    score = tile_scores(query_rows, key_rows)
    return jnp.max(jnp.where(key_pos[None, :] <= query_pos[:, None], score, -jnp.inf), axis=1)


def add_tile(denominator, numerator, query_rows, query_pos, key_rows, value_rows, key_pos, row_top):
    score = tile_scores(query_rows, key_rows)
    allowed = key_pos[None, :] <= query_pos[:, None]
    weights = jnp.where(allowed, jnp.exp(score - row_top[:, None]), 0.0)
    denominator = denominator + jnp.sum(weights, axis=1)
    numerator = numerator + jnp.dot(
        weights.astype(jnp.bfloat16), value_rows, preferred_element_type=jnp.float32
    )
    return (denominator, numerator)


def shards(hidden_in, queries, pair_weight, span_order, yarn_divisor):
    inputs_local = hidden_in[0]
    queries_local = queries[0]
    order_row = span_order[0]
    token_rows = inputs_local.shape[0]
    ulysses_size = lax.axis_size("ulysses")
    cycle_size = lax.axis_size("blk")
    ulysses_index = lax.axis_index("ulysses")
    cycle_index = lax.axis_index("blk")
    block_rows = token_rows * ulysses_size
    span_rows = block_rows // 2
    kv_width = KVH * HD
    group_size = QH // KVH
    own_positions = positions_of(
        order_row, cycle_index * block_rows + ulysses_index * token_rows, token_rows, span_rows
    )
    own_angles = angles(own_positions, yarn_divisor)
    block_positions = positions_of(order_row, cycle_index * block_rows, block_rows, span_rows)
    rotated_queries = rotate(
        queries_local.astype(jnp.float32).reshape(token_rows, QH, HD), own_angles[:, None, :]
    )
    rotated_queries = rotated_queries.astype(jnp.bfloat16).reshape(token_rows, QH * HD)
    projected = jnp.dot(
        inputs_local,
        lax.all_gather(pair_weight, ("dp", "blk"), axis=0, tiled=True),
        preferred_element_type=jnp.float32,
    )
    token_keys = rotate(
        projected[:, :kv_width].reshape(token_rows, KVH, HD), own_angles[:, None, :]
    )
    token_keys = token_keys.astype(jnp.bfloat16).reshape(token_rows, kv_width)
    token_values = projected[:, kv_width:].astype(jnp.bfloat16)
    query_block, key_block, value_block = (
        lax.all_to_all(rotated_queries, "ulysses", split_axis=1, concat_axis=0, tiled=True),
        lax.all_to_all(token_keys, "ulysses", split_axis=1, concat_axis=0, tiled=True),
        lax.all_to_all(token_values, "ulysses", split_axis=1, concat_axis=0, tiled=True),
    )
    own_pair = jnp.stack([key_block, value_block])
    carried_blocks = [own_pair]
    current_pair = own_pair
    for step_index in range(STEPS):
        current_pair = from_behind(current_pair, "blk", 1)
        carried_blocks.append(current_pair)
    carried_positions = []
    for step_index in range(STEPS + 1):
        source_block = jnp.remainder(cycle_index - step_index, cycle_size)
        carried_positions.append(
            positions_of(order_row, source_block * block_rows, block_rows, span_rows)
        )
    output_rows = []
    for query_half in range(2):
        row_start = query_half * span_rows
        half_positions = block_positions[row_start : row_start + span_rows]
        query_pos = jnp.tile(half_positions, group_size)
        query_part = query_block[row_start : row_start + span_rows, 0 : group_size * HD]
        query_rows = (
            query_part.reshape(span_rows, group_size, HD)
            .transpose(1, 0, 2)
            .reshape(group_size * span_rows, HD)
        )
        tile_list = []
        for step_index in range(STEPS + 1):
            pair_block = carried_blocks[step_index]
            for key_half in range(2):
                key_start = key_half * span_rows
                key_rows = pair_block[0, key_start : key_start + span_rows, 0:HD]
                value_rows = pair_block[1, key_start : key_start + span_rows, 0:HD]
                key_pos = carried_positions[step_index][key_start : key_start + span_rows]
                tile_list.append((key_rows, value_rows, key_pos))
        row_top = jnp.full((group_size * span_rows,), -jnp.inf, jnp.float32)
        for key_rows, value_rows, key_pos in tile_list:
            tile_top = row_maximum(query_rows, query_pos, key_rows, key_pos)
            row_top = jnp.maximum(row_top, tile_top)
        denominator = jnp.zeros((group_size * span_rows,), jnp.float32)
        numerator = jnp.zeros((group_size * span_rows, HD), jnp.float32)
        for key_rows, value_rows, key_pos in tile_list:
            denominator, numerator = add_tile(
                denominator,
                numerator,
                query_rows,
                query_pos,
                key_rows,
                value_rows,
                key_pos,
                row_top,
            )
        normalized = (numerator / denominator[:, None]).astype(jnp.bfloat16)
        normalized = (
            normalized.reshape(group_size, span_rows, HD)
            .transpose(1, 0, 2)
            .reshape(span_rows, group_size * HD)
        )
        output_rows.append(normalized)
    block_output = jnp.concatenate(output_rows, axis=0)
    token_output = lax.all_to_all(block_output, "ulysses", split_axis=0, concat_axis=1, tiled=True)
    return token_output[None]


def solution(mesh):
    return jax.shard_map(
        shards,
        mesh=mesh,
        in_specs=(
            P("dp", ("blk", "ulysses"), None),
            P("dp", ("blk", "ulysses"), None),
            P(("dp", "blk"), None),
            P("dp", None),
            P(),
        ),
        out_specs=P("dp", ("blk", "ulysses"), None),
        check_vma=False,
    )
```

profile of v0, /device:TPU:1, one launch (start us, length us, event | category | flops | bytes accessed | tf_op | source)
XLA Modules:
  0.0 342.1 jit_solution(7863774611345590729)
XLA Ops:
  6.5 0.7 all-gather.2.cloned.1.call-update
  7.3 1.2 copy.29
  9.0 0.8 pad_maximum_fusion
  9.9 6.6 %all-to-all-start = ((bf16[128,8,256]{0,2,1:T(8,128)(2,1)}), bf16[128,8,256]{0,2,1:T(8,128)(2,1)S(1)}, u32[]{:S(2)}, u32[]{:S(2)}) async-start(bf16[128,8,256]{0,2,1:T(8,128)(2,1)} %bitcast.2), calls=%async_computation | async-start | bytes 1048576 | tf_op jit(solution)/shard_map/all_to_all | solution.py:106
  17.1 188.4 %all-gather.2.cloned.1.call-done = bf16[4096,2048]{1,0:T(8,128)(2,1)} async-done(((bf16[128,2048]{1,0:T(8,128)(2,1)}), bf16[4096,2048]{1,0:T(8,128)(2,1)}) %all-gather.2.cloned.1.call-update) | async-done | bytes 16777232 | tf_op jit(solution)/shard_map/all_gather | solution.py:97
  205.5 8.1 %fusion.58 = f32[128,2048]{1,0:T(8,128)S(1)} fusion(bf16[4096,2048]{1,0:T(8,128)(2,1)} %all-gather.2.cloned.1.call-done, bf16[1,128,4096]{2,1,0:T(8,128)(2,1)S(1)} %copy-done), kind=kOutput, calls=%fused_computation.98 | convolution fusion | flops 2147483648 | bytes 18874368 | tf_op jit(solution)/shard_map/dot_general | solution.py:95
  214.2 0.8 pad_maximum_fusion.3
  215.0 5.1 %all-to-all-start.1 = ((bf16[128,8,128]{2,0,1:T(8,128)(2,1)}), bf16[128,8,128]{2,0,1:T(8,128)(2,1)S(1)}, u32[]{:S(2)}, u32[]{:S(2)}) async-start(bf16[128,8,128]{2,0,1:T(8,128)(2,1)} %pad_maximum_fusion.3), calls=%async_computation.1 | async-start | bytes 524288 | tf_op jit(solution)/shard_map/all_to_all | solution.py:107
  220.1 0.7 copy_bitcast_fusion
  220.9 5.7 %all-to-all-done.1 = bf16[128,8,128]{2,0,1:T(8,128)(2,1)S(1)} async-done(((bf16[128,8,128]{2,0,1:T(8,128)(2,1)}), bf16[128,8,128]{2,0,1:T(8,128)(2,1)S(1)}, u32[]{:S(2)}, u32[]{:S(2)}) %all-to-all-start.1) | async-done | bytes 262176 | tf_op jit(solution)/shard_map/all_to_all | solution.py:107
  226.6 4.4 %all-to-all-start.2 = ((bf16[128,8,128]{2,0,1:T(8,128)(2,1)}), bf16[128,8,128]{2,0,1:T(8,128)(2,1)S(1)}, u32[]{:S(2)}, u32[]{:S(2)}) async-start(bf16[128,8,128]{2,0,1:T(8,128)(2,1)} %copy_bitcast_fusion), calls=%async_computation.2 | async-start | bytes 524288 | tf_op jit(solution)/shard_map/all_to_all | solution.py:108
  231.5 5.9 %all-to-all-done.2 = bf16[128,8,128]{2,0,1:T(8,128)(2,1)S(1)} async-done(((bf16[128,8,128]{2,0,1:T(8,128)(2,1)}), bf16[128,8,128]{2,0,1:T(8,128)(2,1)S(1)}, u32[]{:S(2)}, u32[]{:S(2)}) %all-to-all-start.2) | async-done | bytes 262176 | tf_op jit(solution)/shard_map/all_to_all | solution.py:108
  237.6 0.4 fusion.126
  238.0 1.8 fusion.125
  239.8 13.8 %collective-permute-done = bf16[2,1024,128]{2,1,0:T(8,128)(2,1)S(1)} collective-permute-done((bf16[2,1024,128]{2,1,0:T(8,128)(2,1)S(1)}, bf16[2,1024,128]{2,1,0:T(8,128)(2,1)S(1)}, u32[]{:S(2)}, u32[]{:S(2)}) %collective-permute-start) | collective-permute-done | bytes 524320 | tf_op jit(solution)/shard_map/ppermute | solution.py:17
  254.5 1.7 fusion.131
  256.7 12.2 %collective-permute-done.1 = bf16[2,1024,128]{2,1,0:T(8,128)(2,1)S(1)} collective-permute-done((bf16[2,1024,128]{2,1,0:T(8,128)(2,1)S(1)}, bf16[2,1024,128]{2,1,0:T(8,128)(2,1)S(1)}, u32[]{:S(2)}, u32[]{:S(2)}) %collective-permute-start.1) | collective-permute-done | bytes 524320 | tf_op jit(solution)/shard_map/ppermute | solution.py:17
  269.7 1.8 fusion.133
  271.5 1.8 fusion.135
  273.3 9.9 %collective-permute-done.2 = bf16[2,1024,128]{2,1,0:T(8,128)(2,1)S(1)} collective-permute-done((bf16[2,1024,128]{2,1,0:T(8,128)(2,1)S(1)}, bf16[2,1024,128]{2,1,0:T(8,128)(2,1)S(1)}, u32[]{:S(2)}, u32[]{:S(2)}) %collective-permute-start.2) | collective-permute-done | bytes 524320 | tf_op jit(solution)/shard_map/ppermute | solution.py:17
  283.2 0.4 fusion.138
  283.6 0.4 fusion.140
  284.1 2.8 fusion.1
  286.9 0.7 fusion.106
  287.5 4.6 %fusion.18 = (f32[1024]{0:T(1024)S(1)}, f32[1024]{0:T(1024)S(1)}, f32[1024]{0:T(1024)S(1)}, f32[1024]{0:T(1024)S(1)}, f32[1024]{0:T(1024)S(1)}, /*index=5*/f32[1024]{0:T(1024)S(1)}, f32[1024]{0:T(1024)S(1)}, f32[1024]{0:T(1024)S(1)}) fusion(f32[1024,512]{0,1:T(8,128)S(1)} %get-tuple-element.63, f32[1024]{0:T(1024)S(1)} %maximum_maximum_fusion.1, ...), kind=kLoop, calls=%fused_computation.50 | loop fusion | flops 20963328 | bytes 16834560 | tf_op jit(solution)/shard_map/reduce_sum | solution.py:66
  292.2 0.7 convolution_add_fusion.7
  292.9 0.7 fusion.104
  293.6 0.7 fusion.102
  294.2 0.7 fusion.100
  294.9 0.7 fusion.48
  295.7 0.7 fusion.49
  296.4 0.7 fusion.57
  297.1 0.9 copy.37
  298.0 1.5 fusion.137
  299.4 1.3 fusion.139
  300.8 5.0 %fusion.9 = (f32[1024]{0:T(1024)S(1)}, f32[1024]{0:T(1024)S(1)}, f32[1024]{0:T(1024)S(1)}, f32[1024]{0:T(1024)S(1)}, f32[1024]{0:T(1024)S(1)}, /*index=5*/f32[10...) fusion(s32[1024]{0:T(1024)S(1)} %bitcast.165, s32[512]{0:T(512)S(1)} %get-tuple-element.53, ...), kind=kOutput, calls=%fused_computation.41 | convolution fusion | flops 150986752 | bytes 17223680 | tf_op jit(solution)/shard_map/dot_general | solution.py:51
  305.8 0.7 fusion.98
  306.5 0.9 copy-done.5
  307.4 4.8 %fusion.34 = (f32[1024]{0:T(1024)S(1)}, f32[1024]{0:T(1024)S(1)}, f32[1024]{0:T(1024)S(1)}, f32[1024]{0:T(1024)S(1)}, f32[1024]{0:T(1024)S(1)}, /*index=5*/f32[1024]{0:T(1024)S(1)}, f32[1024]{0:T(1024)S(1)}, f32[1024]{0:T(1024)S(1)}) fusion(f32[1024,512]{0,1:T(8,128)S(1)} %get-tuple-element.62, f32[1024]{0:T(1024)S(1)} %maximum_maximum_fusion, ...), kind=kLoop, calls=%fused_computation.66 | loop fusion | flops 20963328 | bytes 16834560 | tf_op jit(solution)/shard_map/reduce_sum | solution.py:66
  312.2 0.7 convolution_add_fusion.3
  313.2 0.7 fusion.96
  313.9 0.7 fusion.94
  315.0 0.7 fusion.92
  315.7 0.7 fusion.52
  316.4 0.7 fusion.53
  317.1 0.7 fusion.56
  318.3 15.7 %all_to_all.58 = bf16[8,128,256]{2,1,0:T(8,128)(2,1)S(1)} all-to-all(bf16[8,128,256]{2,1,0:T(8,128)(2,1)S(1)} %bitcast.151), channel_id=1, replica_groups=mesh['dp'=2,'ulysses'=8,'blk'=16] {'ulysses'}, dimensions={0} | all-to-all | bytes 1048576 | tf_op jit(solution)/shard_map/all_to_all | solution.py:167
  334.3 1.0 copy.43
  (85 shorter events, 5.9 us)
Async XLA Ops:
  6.5 199.0 %copy-start = (bf16[1,128,4096]{2,1,0:T(8,128)(2,1)S(1)}, bf16[1,128,4096]{2,1,0:T(8,128)(2,1)}, u32[]{:S(2)}) copy-start(bf16[1,128,4096]{2,1,0:T(8,128)(2,1)} %param.5) | copy-start | bytes 3145732
  6.5 2.0 copy-start.13
  6.5 2.1 copy-start.14
  6.5 199.0 %all-gather.2.cloned.1.call-start = ((), (), s32[]{:S(2)}) async-start(), calls=%async_computation.4 | async-start | bytes 17301504 | tf_op jit(solution)/shard_map/all_gather | solution.py:97
  9.9 205.2 %all-to-all-start = ((bf16[128,8,256]{0,2,1:T(8,128)(2,1)}), bf16[128,8,256]{0,2,1:T(8,128)(2,1)S(1)}, u32[]{:S(2)}, u32[]{:S(2)}) async-start(bf16[128,8,256]{0,2,1:T(8,128)(2,1)} %bitcast.2), calls=%async_computation | async-start | bytes 1048576 | tf_op jit(solution)/shard_map/all_to_all | solution.py:106
  215.0 11.6 %all-to-all-start.1 = ((bf16[128,8,128]{2,0,1:T(8,128)(2,1)}), bf16[128,8,128]{2,0,1:T(8,128)(2,1)S(1)}, u32[]{:S(2)}, u32[]{:S(2)}) async-start(bf16[128,8,128]{2,0,1:T(8,128)(2,1)} %pad_maximum_fusion.3), calls=%async_computation.1 | async-start | bytes 524288 | tf_op jit(solution)/shard_map/all_to_all | solution.py:107
  226.6 10.9 %all-to-all-start.2 = ((bf16[128,8,128]{2,0,1:T(8,128)(2,1)}), bf16[128,8,128]{2,0,1:T(8,128)(2,1)S(1)}, u32[]{:S(2)}, u32[]{:S(2)}) async-start(bf16[128,8,128]{2,0,1:T(8,128)(2,1)} %copy_bitcast_fusion), calls=%async_computation.2 | async-start | bytes 524288 | tf_op jit(solution)/shard_map/all_to_all | solution.py:108
  237.5 16.1 %collective-permute-start = (bf16[2,1024,128]{2,1,0:T(8,128)(2,1)S(1)}, bf16[2,1024,128]{2,1,0:T(8,128)(2,1)S(1)}, u32[]{:S(2)}, u32[]{:S(2)}) collective-permute-start(bf16[2,1024,128]{2,1,0:T(8,128)(2,1)S(1)} %pad_maximum_fusion.1), channel_id=1, source_target_pairs={{15,0},{0,1},{1,2},{2,3},{3,4},{4,5},{5,6},{6,7},{7,8},{8,9},{9,10... | collective-permute-start | bytes 1572872 | tf_op jit(solution)/shard_map/ppermute | solution.py:17
  253.6 41.3 %copy-start.7 = (bf16[2,1024,128]{2,1,0:T(8,128)(2,1)}, bf16[2,1024,128]{2,1,0:T(8,128)(2,1)S(1)}, u32[]{:S(2)}) copy-start(bf16[2,1024,128]{2,1,0:T(8,128)(2,1)S(1)} %collective-permute-done) | copy-start | bytes 1572868
  253.6 15.2 %collective-permute-start.1 = (bf16[2,1024,128]{2,1,0:T(8,128)(2,1)S(1)}, bf16[2,1024,128]{2,1,0:T(8,128)(2,1)S(1)}, u32[]{:S(2)}, u32[]{:S(2)}) collective-permute-start(bf16[2,1024,128]{2,1,0:T(8,128)(2,1)S(1)} %collective-permute-done), channel_id=1, source_target_pairs={{15,0},{0,1},{1,2},{2,3},{3,4},{4,5},{5,6},{6,7},{7,8},{8,9},{9,10... | collective-permute-start | bytes 1572872 | tf_op jit(solution)/shard_map/ppermute | solution.py:17
  268.8 26.8 %copy-start.9 = (bf16[2,1024,128]{2,1,0:T(8,128)(2,1)}, bf16[2,1024,128]{2,1,0:T(8,128)(2,1)S(1)}, u32[]{:S(2)}) copy-start(bf16[2,1024,128]{2,1,0:T(8,128)(2,1)S(1)} %collective-permute-done.1) | copy-start | bytes 1572868
  268.8 14.3 %collective-permute-start.2 = (bf16[2,1024,128]{2,1,0:T(8,128)(2,1)S(1)}, bf16[2,1024,128]{2,1,0:T(8,128)(2,1)S(1)}, u32[]{:S(2)}, u32[]{:S(2)}) collective-permute-start(bf16[2,1024,128]{2,1,0:T(8,128)(2,1)S(1)} %collective-permute-done.1), channel_id=1, source_target_pairs={{15,0},{0,1},{1,2},{2,3},{3,4},{4,5},{5,6},{6,7},{7,8},{8,9},{9,10... | collective-permute-start | bytes 1572872 | tf_op jit(solution)/shard_map/ppermute | solution.py:17
  283.2 13.2 %copy-start.11 = (bf16[2,1024,128]{2,1,0:T(8,128)(2,1)}, bf16[2,1024,128]{2,1,0:T(8,128)(2,1)S(1)}, u32[]{:S(2)}) copy-start(bf16[2,1024,128]{2,1,0:T(8,128)(2,1)S(1)} %collective-permute-done.2) | copy-start | bytes 1572868
  297.9 2.8 copy-start.2
  297.9 2.8 copy-start.3
  300.8 5.0 %copy-start.4 = (f32[1024,512]{0,1:T(8,128)S(1)}, f32[1024,512]{0,1:T(8,128)}, u32[]{:S(2)}) copy-start(f32[1024,512]{0,1:T(8,128)} %fusion.125) | copy-start | bytes 6291460
  305.8 1.6 copy-start.5
  312.2 1.0 copy-start.8
  312.9 1.1 copy-start.10
  313.9 1.0 copy-start.12
  317.0 1.0 copy-start.6
  318.0 17.3 %copy-start.1 = (bf16[1,128,4096]{2,1,0:T(8,128)(2,1)S(1)}, bf16[1,128,4096]{2,1,0:T(8,128)(2,1)}, u32[]{:S(2)}) copy-start(bf16[1,128,4096]{2,1,0:T(8,128)(2,1)} %param.5) | copy-start | bytes 3145732
Sparse Core Ops, SparseCore 0:
  9.1 196.3 all-gather.1
where the time goes:
time: 343 us; the launch traced here: 342 us
  waiting for transfers between devices  237 us (69%)
  matrix products  40.2 us (12%)
  starting transfers between devices  16.1 us (5%)
  blocking collectives  15.7 us (5%)
  between operations  14 us (4%)
  other arithmetic  12.2 us (4%)
  local copies, waits for them, and re-layouts  7.27 us (2%)
    all_gather x1, waiting for transfers between devices, shards(): lax.all_gather(pair_weight, ('dp', 'blk'), axis=0, tiled=True)  188 us
    ppermute x3, waiting for transfers between devices, from_behind(): return lax.ppermute(block, axis, route)  35.9 us
    dot_general x16, matrix products, tile_scores(): lax.dot_general(query_rows, key_rows, (((1,), (1,)), ((), ())), preferred...  21.1 us
    all_to_all x1, blocking collectives, shards(): lax.all_to_all(block_output, 'ulysses', split_axis=0, concat_axis=1, tile...  15.7 us
    dot_general x16, matrix products, add_tile(): jnp.dot(weights.astype(jnp.bfloat16), value_rows, preferred_element_type=...  11 us
    reduce_sum x2, other arithmetic, add_tile(): denominator = denominator + jnp.sum(weights, axis=1)  9.41 us
    dot_general x1, matrix products, shards(): jnp.dot(inputs_local, lax.all_gather(pair_weight, ('dp', 'blk'), axis=0,...  8.1 us
  transfers between devices with their start and end apart: 7, of which 6 were waited for; matrix products, arithmetic and copies ran while one was open for 7% of the time, Pallas kernels for 0%

commit v1 on v0

--- a/solution.py
+++ b/solution.py
@@ -1,14 +1,31 @@
+import functools
 import math
 import jax
 import jax.numpy as jnp
 from jax import lax
 from jax.sharding import PartitionSpec as P
+from jax.lax import all_to_all, axis_size
 
 KVH = 8
 HD = 128
 QH = 16
 STEPS = 3
 LOG_BASE = math.log(500000.0)
+
+
+def handle_the_ladders(vec, comm_axis, along_dim):
+    return jnp.concatenate(
+        all_to_all(
+            jnp.stack([vec for _ in range(axis_size(comm_axis))]),
+            split_axis=0,
+            axis_name=comm_axis,
+            concat_axis=0,
+        ),
+        along_dim,
+    )
+
+
+_find_pipes = functools.partial(handle_the_ladders, comm_axis=("dp", "blk"), along_dim=0)
 
 
 def from_behind(block, axis, distance):
@@ -92,11 +109,7 @@
         queries_local.astype(jnp.float32).reshape(token_rows, QH, HD), own_angles[:, None, :]
     )
     rotated_queries = rotated_queries.astype(jnp.bfloat16).reshape(token_rows, QH * HD)
-    projected = jnp.dot(
-        inputs_local,
-        lax.all_gather(pair_weight, ("dp", "blk"), axis=0, tiled=True),
-        preferred_element_type=jnp.float32,
-    )
+    projected = jnp.dot(inputs_local, _find_pipes(pair_weight), preferred_element_type=jnp.float32)
     token_keys = rotate(
         projected[:, :kv_width].reshape(token_rows, KVH, HD), own_angles[:, None, :]
     )

time: 343 us -> 550 us (1.60)
  waiting for transfers between devices: 237 us -> 440 us
  between operations: 14 us -> 0.64 us
  starting transfers between devices: 16.1 us -> 27.4 us
  local copies, waits for them, and re-layouts: 7.27 us -> 13.1 us
    all_to_all x0 -> x1, waiting for transfers between devices: none -> 392 us  [handle_the_ladders(): all_to_all(jnp.stack([vec for _ in range(axis_size(comm_axis))]), split_a...]
    all_gather x1 -> x0, waiting for transfers between devices: 188 us -> none  [shards(): lax.all_gather(pair_weight, ('dp', 'blk'), axis=0, tiled=True)]
    all_to_all x0 -> x1, starting transfers between devices: none -> 12.3 us  [handle_the_ladders(): all_to_all(jnp.stack([vec for _ in range(axis_size(comm_axis))]), split_a...]
    another operation x0 -> x1, local copies, waits for them, and re-layouts: none -> 6.88 us  [handle_the_ladders(): jnp.stack([vec for _ in range(axis_size(comm_axis))])]
  transfers between devices with their start and end apart: 7 -> 7, of which waited for: 6 -> 6; matrix products, arithmetic and copies ran while one was open for 7% -> 4% of each run, Pallas kernels for 0% -> 0%
where the time goes in v1:
time: 550 us; the launch traced here: 549 us
  waiting for transfers between devices  440 us (80%)
  matrix products  40.2 us (7%)
  starting transfers between devices  27.4 us (5%)
  blocking collectives  15.7 us (3%)
  local copies, waits for them, and re-layouts  13.1 us (2%)
  other arithmetic  12.2 us (2%)
    all_to_all x1, waiting for transfers between devices, handle_the_ladders(): all_to_all(jnp.stack([vec for _ in range(axis_size(comm_axis))]), split_a...  392 us
    ppermute x3, waiting for transfers between devices, from_behind(): return lax.ppermute(block, axis, route)  35.9 us
    dot_general x16, matrix products, tile_scores(): lax.dot_general(query_rows, key_rows, (((1,), (1,)), ((), ())), preferred...  21.1 us
    all_to_all x1, blocking collectives, shards(): lax.all_to_all(block_output, 'ulysses', split_axis=0, concat_axis=1, tile...  15.7 us
    all_to_all x1, starting transfers between devices, handle_the_ladders(): all_to_all(jnp.stack([vec for _ in range(axis_size(comm_axis))]), split_a...  12.3 us
  transfers between devices with their start and end apart: 7, of which 6 were waited for; matrix products, arithmetic and copies ran while one was open for 4% of the time, Pallas kernels for 0%

profile of v1, /device:TPU:1, one launch (start us, length us, event | category | flops | bytes accessed | tf_op | source)
XLA Modules:
  0.0 549.1 jit_solution(13541874149968024617)
XLA Ops:
  0.0 6.9 %stack.8 = bf16[32,128,2048]{2,1,0:T(8,128)(2,1)} broadcast(bf16[128,2048]{1,0:T(8,128)(2,1)} %param.7), dimensions={1,2} | broadcast | bytes 17301504 | tf_op jit(solution)/shard_map/stack | solution.py:19
  6.9 12.3 %all-to-all-start.1 = ((bf16[32,128,2048]{2,1,0:T(8,128)(2,1)}), bf16[32,128,2048]{2,1,0:T(8,128)(2,1)}, u32[]{:S(2)}, u32[]{:S(2)}) async-start(bf16[32,128,2048]{2,1,0:T(8,128)(2,1)} %stack.8), calls=%async_computation.1 | async-start | bytes 33554432 | tf_op jit(solution)/shard_map/all_to_all | solution.py:18
  20.5 0.8 pad_maximum_fusion
  21.5 392.4 %all-to-all-done.1 = bf16[32,128,2048]{2,1,0:T(8,128)(2,1)} async-done(((bf16[32,128,2048]{2,1,0:T(8,128)(2,1)}), bf16[32,128,2048]{2,1,0:T(8,128)(2,1)}, u32[]{:S(2)}, u32[]{:S(2)}) %all-to-all-start.1) | async-done | bytes 16777248 | tf_op jit(solution)/shard_map/all_to_all | solution.py:18
  413.9 5.8 %all-to-all-start = ((bf16[128,8,256]{0,2,1:T(8,128)(2,1)}), bf16[128,8,256]{0,2,1:T(8,128)(2,1)S(1)}, u32[]{:S(2)}, u32[]{:S(2)}) async-start(bf16[128,8,256]{0,2,1:T(8,128)(2,1)} %bitcast.2), calls=%async_computation | async-start | bytes 1048576 | tf_op jit(solution)/shard_map/all_to_all | solution.py:119
  419.7 8.1 %fusion.58 = f32[128,2048]{1,0:T(8,128)S(1)} fusion(bf16[4096,2048]{1,0:T(8,128)(2,1)} %bitcast.7, bf16[1,128,4096]{2,1,0:T(8,128)(2,1)S(1)} %copy-done), kind=kOutput, calls=%fused_computation.98 | convolution fusion | flops 2147483648 | bytes 18874368 | tf_op jit(solution)/shard_map/dot_general | solution.py:112
  428.4 0.8 pad_maximum_fusion.3
  429.2 4.8 all-to-all-start.2
  434.0 0.7 copy_bitcast_fusion
  434.7 5.7 %all-to-all-done.2 = bf16[128,8,128]{2,0,1:T(8,128)(2,1)S(1)} async-done(((bf16[128,8,128]{2,0,1:T(8,128)(2,1)}), bf16[128,8,128]{2,0,1:T(8,128)(2,1)S(1)}, u32[]{:S(2)}, u32[]{:S(2)}) %all-to-all-start.2) | async-done | bytes 262176 | tf_op jit(solution)/shard_map/all_to_all | solution.py:120
  440.5 4.4 all-to-all-start.3
  445.4 5.9 %all-to-all-done.3 = bf16[128,8,128]{2,0,1:T(8,128)(2,1)S(1)} async-done(((bf16[128,8,128]{2,0,1:T(8,128)(2,1)}), bf16[128,8,128]{2,0,1:T(8,128)(2,1)S(1)}, u32[]{:S(2)}, u32[]{:S(2)}) %all-to-all-start.3) | async-done | bytes 262176 | tf_op jit(solution)/shard_map/all_to_all | solution.py:121
  451.5 0.4 fusion.126
  451.9 1.8 fusion.125
  453.7 13.8 %collective-permute-done = bf16[2,1024,128]{2,1,0:T(8,128)(2,1)S(1)} collective-permute-done((bf16[2,1024,128]{2,1,0:T(8,128)(2,1)S(1)}, bf16[2,1024,128]{2,1,0:T(8,128)(2,1)S(1)}, u32[]{:S(2)}, u32[]{:S(2)}) %collective-permute-start) | collective-permute-done | bytes 524320 | tf_op jit(solution)/shard_map/ppermute | solution.py:34
  468.0 0.4 fusion.132
  468.4 1.7 fusion.131
  470.6 12.2 %collective-permute-done.1 = bf16[2,1024,128]{2,1,0:T(8,128)(2,1)S(1)} collective-permute-done((bf16[2,1024,128]{2,1,0:T(8,128)(2,1)S(1)}, bf16[2,1024,128]{2,1,0:T(8,128)(2,1)S(1)}, u32[]{:S(2)}, u32[]{:S(2)}) %collective-permute-start.1) | collective-permute-done | bytes 524320 | tf_op jit(solution)/shard_map/ppermute | solution.py:34
  483.2 0.4 fusion.136
  483.6 1.8 fusion.133
  485.4 1.8 fusion.135
  487.1 9.9 %collective-permute-done.2 = bf16[2,1024,128]{2,1,0:T(8,128)(2,1)S(1)} collective-permute-done((bf16[2,1024,128]{2,1,0:T(8,128)(2,1)S(1)}, bf16[2,1024,128]{2,1,0:T(8,128)(2,1)S(1)}, u32[]{:S(2)}, u32[]{:S(2)}) %collective-permute-start.2) | collective-permute-done | bytes 524320 | tf_op jit(solution)/shard_map/ppermute | solution.py:34
  497.9 2.8 fusion.1
  500.7 0.7 fusion.106
  501.4 4.6 fusion.18
  506.0 0.7 convolution_add_fusion.7
  506.8 0.7 fusion.104
  507.4 0.7 fusion.102
  508.1 0.7 fusion.100
  508.8 0.7 fusion.48
  509.5 0.7 fusion.49
  510.2 0.7 fusion.57
  511.0 0.9 copy.37
  511.8 1.5 fusion.137
  513.3 1.3 fusion.139
  514.7 5.0 fusion.9
  519.7 0.7 fusion.98
  520.4 0.9 copy-done.5
  521.2 4.8 fusion.34
  526.0 0.7 convolution_add_fusion.3
  527.1 0.7 fusion.96
  527.8 0.7 fusion.94
  528.9 0.7 fusion.92
  529.5 0.7 fusion.52
  530.2 0.7 fusion.53
  530.9 0.7 fusion.56
  532.1 15.7 %all_to_all.63 = bf16[8,128,256]{2,1,0:T(8,128)(2,1)S(1)} all-to-all(bf16[8,128,256]{2,1,0:T(8,128)(2,1)S(1)} %bitcast.152), channel_id=1, replica_groups=mesh['dp'=2,'ulysses'=8,'blk'=16] {'ulysses'}, dimensions={0} | all-to-all | bytes 1048576 | tf_op jit(solution)/shard_map/all_to_all | solution.py:180
  548.1 1.0 copy.43
  (87 shorter events, 6.1 us)
Async XLA Ops:
  0.0 419.7 %copy-start = (bf16[1,128,4096]{2,1,0:T(8,128)(2,1)S(1)}, bf16[1,128,4096]{2,1,0:T(8,128)(2,1)}, u32[]{:S(2)}) copy-start(bf16[1,128,4096]{2,1,0:T(8,128)(2,1)} %param.5) | copy-start | bytes 3145732
  6.9 12.5 %copy-start.14 = (s32[1,32]{1,0:T(1,128)S(1)}, s32[1,32]{1,0:T(1,128)}, u32[]{:S(2)}) copy-start(s32[1,32]{1,0:T(1,128)} %param.8) | copy-start | bytes 388
  6.9 12.8 %copy-start.15 = (s32[64]{0:T(128)S(1)}, s32[64]{0:T(128)}, u32[]{:S(2)}) copy-start(s32[64]{0:T(128)} %param.9) | copy-start | bytes 772
  6.9 13.3 %copy-start.7 = (bf16[1,128,2048]{2,1,0:T(8,128)(2,1)S(1)}, bf16[1,128,2048]{2,1,0:T(8,128)(2,1)}, u32[]{:S(2)}) copy-start(bf16[1,128,2048]{2,1,0:T(8,128)(2,1)} %param.6) | copy-start | bytes 1572868
  6.9 407.0 %all-to-all-start.1 = ((bf16[32,128,2048]{2,1,0:T(8,128)(2,1)}), bf16[32,128,2048]{2,1,0:T(8,128)(2,1)}, u32[]{:S(2)}, u32[]{:S(2)}) async-start(bf16[32,128,2048]{2,1,0:T(8,128)(2,1)} %stack.8), calls=%async_computation.1 | async-start | bytes 33554432 | tf_op jit(solution)/shard_map/all_to_all | solution.py:18
  413.9 15.3 %all-to-all-start = ((bf16[128,8,256]{0,2,1:T(8,128)(2,1)}), bf16[128,8,256]{0,2,1:T(8,128)(2,1)S(1)}, u32[]{:S(2)}, u32[]{:S(2)}) async-start(bf16[128,8,256]{0,2,1:T(8,128)(2,1)} %bitcast.2), calls=%async_computation | async-start | bytes 1048576 | tf_op jit(solution)/shard_map/all_to_all | solution.py:119
  429.2 11.3 %all-to-all-start.2 = ((bf16[128,8,128]{2,0,1:T(8,128)(2,1)}), bf16[128,8,128]{2,0,1:T(8,128)(2,1)S(1)}, u32[]{:S(2)}, u32[]{:S(2)}) async-start(bf16[128,8,128]{2,0,1:T(8,128)(2,1)} %pad_maximum_fusion.3), calls=%async_computation.2 | async-start | bytes 524288 | tf_op jit(solution)/shard_map/all_to_all | solution.py:120
  440.5 10.9 %all-to-all-start.3 = ((bf16[128,8,128]{2,0,1:T(8,128)(2,1)}), bf16[128,8,128]{2,0,1:T(8,128)(2,1)S(1)}, u32[]{:S(2)}, u32[]{:S(2)}) async-start(bf16[128,8,128]{2,0,1:T(8,128)(2,1)} %copy_bitcast_fusion), calls=%async_computation.3 | async-start | bytes 524288 | tf_op jit(solution)/shard_map/all_to_all | solution.py:121
  451.4 16.1 %collective-permute-start = (bf16[2,1024,128]{2,1,0:T(8,128)(2,1)S(1)}, bf16[2,1024,128]{2,1,0:T(8,128)(2,1)S(1)}, u32[]{:S(2)}, u32[]{:S(2)}) collective-permute-start(bf16[2,1024,128]{2,1,0:T(8,128)(2,1)S(1)} %pad_maximum_fusion.1), channel_id=1, source_target_pairs={{15,0},{0,1},{1,2},{2,3},{3,4},{4,5},{5,6},{6,7},{7,8},{8,9},{9,10... | collective-permute-start | bytes 1572872 | tf_op jit(solution)/shard_map/ppermute | solution.py:34
  467.5 41.3 %copy-start.8 = (bf16[2,1024,128]{2,1,0:T(8,128)(2,1)}, bf16[2,1024,128]{2,1,0:T(8,128)(2,1)S(1)}, u32[]{:S(2)}) copy-start(bf16[2,1024,128]{2,1,0:T(8,128)(2,1)S(1)} %collective-permute-done) | copy-start | bytes 1572868
  467.5 15.2 %collective-permute-start.1 = (bf16[2,1024,128]{2,1,0:T(8,128)(2,1)S(1)}, bf16[2,1024,128]{2,1,0:T(8,128)(2,1)S(1)}, u32[]{:S(2)}, u32[]{:S(2)}) collective-permute-start(bf16[2,1024,128]{2,1,0:T(8,128)(2,1)S(1)} %collective-permute-done), channel_id=1, source_target_pairs={{15,0},{0,1},{1,2},{2,3},{3,4},{4,5},{5,6},{6,7},{7,8},{8,9},{9,10... | collective-permute-start | bytes 1572872 | tf_op jit(solution)/shard_map/ppermute | solution.py:34
  482.7 26.8 %copy-start.10 = (bf16[2,1024,128]{2,1,0:T(8,128)(2,1)}, bf16[2,1024,128]{2,1,0:T(8,128)(2,1)S(1)}, u32[]{:S(2)}) copy-start(bf16[2,1024,128]{2,1,0:T(8,128)(2,1)S(1)} %collective-permute-done.1) | copy-start | bytes 1572868
  482.7 14.3 %collective-permute-start.2 = (bf16[2,1024,128]{2,1,0:T(8,128)(2,1)S(1)}, bf16[2,1024,128]{2,1,0:T(8,128)(2,1)S(1)}, u32[]{:S(2)}, u32[]{:S(2)}) collective-permute-start(bf16[2,1024,128]{2,1,0:T(8,128)(2,1)S(1)} %collective-permute-done.1), channel_id=1, source_target_pairs={{15,0},{0,1},{1,2},{2,3},{3,4},{4,5},{5,6},{6,7},{7,8},{8,9},{9,10... | collective-permute-start | bytes 1572872 | tf_op jit(solution)/shard_map/ppermute | solution.py:34
  497.1 13.2 %copy-start.12 = (bf16[2,1024,128]{2,1,0:T(8,128)(2,1)}, bf16[2,1024,128]{2,1,0:T(8,128)(2,1)S(1)}, u32[]{:S(2)}) copy-start(bf16[2,1024,128]{2,1,0:T(8,128)(2,1)S(1)} %collective-permute-done.2) | copy-start | bytes 1572868
  511.8 2.8 copy-start.2
  511.8 2.8 copy-start.3
  514.7 5.0 copy-start.4
  519.6 1.6 copy-start.5
  526.0 1.0 copy-start.9
  526.7 1.1 copy-start.11
  527.8 1.0 copy-start.13
  530.9 1.0 copy-start.6
  531.9 17.3 %copy-start.1 = (bf16[1,128,4096]{2,1,0:T(8,128)(2,1)S(1)}, bf16[1,128,4096]{2,1,0:T(8,128)(2,1)}, u32[]{:S(2)}) copy-start(bf16[1,128,4096]{2,1,0:T(8,128)(2,1)} %param.5) | copy-start | bytes 3145732
